TPU v7x, 512 devices: a whole 4x4x16 slice. The times are simulated.
512 devices in a mesh: wide: 128 (over z, y, core), narrow: 4 (over x).
Axes of the slice: x: 4, y: 4, z: 16, core: 2. Of those that a mesh axis runs over, the one named last changes fastest.
Arguments:
- tokens: bfloat16 [1024, 1024], P('wide', 'narrow'), may hold values from -6 to 6
- norm_gain: float32 [1024], replicated, may hold values from 0.1 to 1.9
- w_qk: bfloat16 [1024, 2, 1024], P(None, None, 'narrow'), may hold values from -0.0625 to 0.0625
- w_value: bfloat16 [1024, 1024], P(None, 'narrow'), may hold values from -0.1875 to 0.1875
- w_out: bfloat16 [1024, 1024], P('narrow'), may hold values from -1.5 to 1.5
- kv_cache: bfloat16 [8192, 2, 32, 1024], P('wide', None, None, 'narrow'), may hold values from -200 to 200
- cache_len: int32 [1024], replicated, may hold values from 1 to 256, as said below
- page_table: int32 [1024, 8], replicated, may hold values from 0 to 63, as said below
Outputs:
- attended: bfloat16 [1024, 1024], P('wide', 'narrow')
Inputs may be any that keep to these rules, and one draw needn't show every extreme that they name: `cache_len`: every request has one or more cached positions, and some request has exactly 256. `page_table`: on every owner, the pairs (request, page) placed there by the rule of the steps occupy its 64 slots one to one.
All inputs are finite; a program needn't handle non-finite values.
Results may differ from a plain program's by a relative error of at most 0.015.
The roundings to bfloat16 on the way count: a program that leaves them out, or rounds other values in their place, can miss the bound.
Values may be sent and summed in bfloat16 or wider, within the bound.
A program may use at most 64 MiB of HBM per device.

v0:
```python
import jax
import jax.numpy as jnp
from jax import lax
from jax.sharding import PartitionSpec as P

HEAD_DIM = 64


def page_partial(query_rows, request_rows, page_rows, kv_cache, cache_len, page_table):
    count = query_rows.shape[0]
    width = query_rows.shape[1]
    local_heads = width // HEAD_DIM
    page_len = kv_cache.shape[2]
    slot_rows = page_table[request_rows, page_rows]
    lengths = cache_len[request_rows]
    keys = kv_cache[slot_rows, 0].reshape(count, page_len, local_heads, HEAD_DIM)
    values = kv_cache[slot_rows, 1].reshape(count, page_len, local_heads, HEAD_DIM)
    q_heads = query_rows.reshape(count, local_heads, HEAD_DIM)
    scores = jnp.einsum("nhe,nphe->nhp", q_heads, keys, preferred_element_type=jnp.float32)
    places = page_rows[:, None] * page_len + jnp.arange(page_len, dtype=jnp.int32)[None, :]
    valid = (places < lengths[:, None])[:, None, :]
    scores = jnp.where(valid, scores, -1e30)
    page_max = jnp.max(scores, axis=-1)
    weights = jnp.where(valid, jnp.exp(scores - page_max[..., None]), 0.0)
    page_sum = jnp.sum(weights, axis=-1)
    page_acc = jnp.einsum(
        "nhp,nphe->nhe", weights.astype(jnp.bfloat16), values, preferred_element_type=jnp.float32
    )
    return (page_max, page_sum, page_acc.reshape(count, width))


def body(tokens, norm_gain, w_qk, w_value, w_out, kv_cache, cache_len, page_table):
    gathered = lax.all_gather(tokens, "narrow", axis=1, tiled=True)
    floats = gathered.astype(jnp.float32)
    normed = (
        floats * lax.rsqrt(jnp.mean(floats * floats, axis=-1, keepdims=True) + 1e-06) * norm_gain
    ).astype(jnp.bfloat16)
    both = jnp.einsum("td,dcf->tcf", normed, w_qk, preferred_element_type=jnp.float32).astype(
        jnp.bfloat16
    )
    own_queries = both[:, 0, :]
    new_keys = both[:, 1, :]
    new_values = jnp.dot(normed, w_value, preferred_element_type=jnp.float32).astype(jnp.bfloat16)
    tok_count = tokens.shape[0]
    width = own_queries.shape[1]
    local_heads = width // HEAD_DIM
    page_count = page_table.shape[1]
    wide_count = lax.axis_size("wide")
    stride_len = wide_count // page_count
    my_index = lax.axis_index("wide")
    local_ids = jnp.arange(tok_count, dtype=jnp.int32)
    self_score = jnp.sum(
        own_queries.reshape(tok_count, local_heads, HEAD_DIM).astype(jnp.float32)
        * new_keys.reshape(tok_count, local_heads, HEAD_DIM).astype(jnp.float32),
        axis=-1,
    )
    value_heads = new_values.reshape(tok_count, local_heads, HEAD_DIM).astype(jnp.float32)
    all_queries = lax.all_gather(own_queries, "wide", axis=0, tiled=True)
    page_rows = jnp.repeat(jnp.arange(page_count, dtype=jnp.int32), tok_count)
    slot_local = jnp.tile(local_ids, page_count)
    page_offsets = (page_rows - page_rows % 2) * stride_len + page_rows % 2
    home_rows = (my_index - page_offsets) % wide_count
    request_rows = home_rows * tok_count + slot_local
    page_max, page_sum, page_acc = page_partial(
        all_queries[request_rows], request_rows, page_rows, kv_cache, cache_len, page_table
    )
    total = wide_count * tok_count
    max_table = jnp.full((total, local_heads), -1e30, jnp.float32).at[request_rows].set(page_max)
    best = lax.pmax(max_table, "wide")
    factor = jnp.exp(page_max - best[request_rows])
    scaled = (page_acc.reshape(-1, local_heads, HEAD_DIM) * factor[..., None]).reshape(-1, width)
    numer_table = jnp.zeros((total, width), jnp.float32).at[request_rows].set(scaled)
    denom_table = (
        jnp.zeros((total, local_heads), jnp.float32).at[request_rows].set(page_sum * factor)
    )
    numer, denom = (
        lax.psum_scatter(numer_table, "wide", scatter_dimension=0, tiled=True),
        lax.psum_scatter(denom_table, "wide", scatter_dimension=0, tiled=True),
    )
    best_home = lax.dynamic_slice_in_dim(best, my_index * tok_count, tok_count, 0)
    top = jnp.maximum(best_home, self_score)
    rescale = jnp.exp(best_home - top)
    self_factor = jnp.exp(self_score - top)
    numer = (
        numer.reshape(tok_count, local_heads, HEAD_DIM) * rescale[..., None]
        + self_factor[..., None] * value_heads
    )
    denom = denom * rescale + self_factor
    heads_out = (numer / denom[..., None]).reshape(tok_count, width).astype(jnp.bfloat16)
    partial_out = jnp.dot(heads_out, w_out, preferred_element_type=jnp.float32)
    return lax.psum_scatter(partial_out, "narrow", scatter_dimension=1, tiled=True).astype(
        jnp.bfloat16
    )


def solution(mesh):
    placed = (
        P("wide", "narrow"),
        P(),
        P(None, None, "narrow"),
        P(None, "narrow"),
        P("narrow", None),
        P("wide", None, None, "narrow"),
        P(),
        P(),
    )
    return jax.shard_map(
        body, mesh=mesh, in_specs=placed, out_specs=P("wide", "narrow"), check_vma=False
    )
```

profile of v0, /device:TPU:8, one launch (start us, length us, event | category | flops | bytes accessed | tf_op | source)
XLA Modules:
  0.0 1149.0 jit_solution(1433137674564910092)
XLA Ops:
  6.7 12.5 %all_gather.6 = bf16[8,1024]{1,0:T(8,128)(2,1)S(1)} all-gather(bf16[8,256]{1,0:T(8,128)(2,1)} %param.8), channel_id=1, replica_groups=mesh['wide'=128,'narrow'=4] {'narrow'}, dimensions={1}, use_global_device_ids=true | all-gather | bytes 20480 | tf_op jit(solution)/shard_map/all_gather | solution.py:33
  19.4 1.5 convolution_convert_fusion
  20.9 89.3 %all-gather = bf16[1024,1,256]{2,0,1:T(8,128)(2,1)S(1)} all-gather(bf16[8,1,256]{2,0,1:T(8,128)(2,1)S(1)} %slice.20), channel_id=2, replica_groups=mesh['wide'=128,'narrow'=4] {'wide'}, dimensions={0}, use_global_device_ids=true | all-gather | bytes 528384 | tf_op jit(solution)/shard_map/all_gather | solution.py:58
  110.3 0.7 gather_fusion.1
  111.1 0.8 gather_fusion.2
  111.9 0.7 gather_fusion.3
  112.6 1.9 reshape.247
  114.5 2.8 fusion.2
  117.4 0.7 gather_fusion
  118.4 0.9 scatter_custom_fusion
  119.3 488.9 %pmax.7 = f32[1024,4]{1,0:T(8,128)S(1)} all-reduce(f32[1024,4]{1,0:T(8,128)S(1)} %scatter_custom_fusion), channel_id=1, replica_groups=mesh['wide'=128,'narrow'=4] {'wide'}, use_global_device_ids=true, to_apply=%region_3.4 | all-reduce | flops 4096 | bytes 32768 | tf_op jit(solution)/shard_map/pmax | solution.py:69
  608.3 0.6 gather_fusion.5
  609.1 0.7 gather_fusion.4
  609.8 1.9 reshape.248
  611.8 2.2 fusion
  614.0 0.1 broadcast_multiply_fusion
  614.3 1.8 scatter_custom_fusion.1
  616.3 0.9 scatter_custom_fusion.2
  617.4 1.3 dynamic-slice
  619.3 491.0 %all-reduce.2 = f32[1024,4]{1,0:T(8,128)S(1)} all-reduce(f32[1024,4]{1,0:T(8,128)S(1)} %scatter_custom_fusion.2), channel_id=4, replica_groups=mesh['wide'=128,'narrow'=4] {'wide'}, use_global_device_ids=true, to_apply=%region_9.10.clone | all-reduce | flops 4096 | bytes 32768
  1110.2 0.7 fusion.28
  1111.4 2.3 fusion.9
  1113.8 27.1 %reduce-scatter.5.cloned.1.call-done = f32[8,256]{1,0:T(8,128)} async-done(((f32[8,1024]{1,0:T(8,128)}), f32[8,256]{1,0:T(8,128)}) %reduce-scatter.5.cloned.1.call-update) | async-done | bytes 8208 | tf_op jit(solution)/shard_map/reduce_scatter | solution.py:91
  1140.9 1.3 convert_element_type.50
  (48 shorter events, 2.1 us)
Async XLA Ops:
  6.5 105.4 %copy-start = (bf16[64,2,32,256]{3,2,1,0:T(8,128)(2,1)S(1)}, bf16[64,2,32,256]{3,2,1,0:T(8,128)(2,1)}, u32[]{:S(2)}) copy-start(bf16[64,2,32,256]{3,2,1,0:T(8,128)(2,1)} %param.13) | copy-start | bytes 6291460
  6.5 104.5 %copy-start.2 = (s32[1024,8]{0,1:T(8,128)S(1)}, s32[1024,8]{0,1:T(8,128)}, u32[]{:S(2)}) copy-start(s32[1024,8]{0,1:T(8,128)} %param.15) | copy-start | bytes 98308
  6.5 1104.9 %reduce-scatter.3.cloned.1.call-start = ((), (), s32[]{:S(2)}) async-start(), calls=%async_computation.2 | async-start | bytes 1056768 | tf_op jit(solution)/shard_map/reduce_scatter | solution.py:77
  114.5 2.9 copy-start.1
  608.3 0.8 copy-start.3
  614.2 497.2 %copy-start.4 = (f32[1024]{0:T(1024)S(1)}, f32[1024]{0:T(1024)}, u32[]{:S(2)}) copy-start(f32[1024]{0:T(1024)} %param.9) | copy-start | bytes 12292
  616.2 524.7 %reduce-scatter.5.cloned.1.call-start = ((), (), s32[]{:S(2)}) async-start(), calls=%async_computation.3 | async-start | bytes 40960 | tf_op jit(solution)/shard_map/reduce_scatter | solution.py:91
Sparse Core Ops, SparseCore 0:
  616.3 258.9 reduce-scatter.2
  1113.9 26.9 reduce-scatter.4
where the time goes:
time: 1150 us
  blocking collectives  1080 us (94%)
  waiting for transfers between devices  27.2 us (2%)
  local copies, waits for them, and re-layouts  14.5 us (1%)
  between operations  14.2 us (1%)
    unnamed x1, blocking collectives  491 us
    pmax x1, blocking collectives, body(): best = lax.pmax(max_table, 'wide')  489 us
    all_gather x1, blocking collectives, body(): all_queries = lax.all_gather(own_queries, 'wide', axis=0, tiled=True)  89.3 us
    reduce_scatter x1, waiting for transfers between devices, body(): lax.psum_scatter(partial_out, 'narrow', scatter_dimension=1, tiled=True)  27.1 us
  transfers between devices with their start and end apart: 2, of which 1 were waited for; matrix products, arithmetic and copies ran while one was open for 0% of the time, Pallas kernels for 0%

commit v1 on v0

--- a/solution.py
+++ b/solution.py
@@ -55,7 +55,10 @@
         axis=-1,
     )
     value_heads = new_values.reshape(tok_count, local_heads, HEAD_DIM).astype(jnp.float32)
-    all_queries = lax.all_gather(own_queries, "wide", axis=0, tiled=True)
+    mixed_arr = tuple((own_queries for _ in range(lax.psum(1, "wide"))))
+    outer = jnp.stack(mixed_arr)
+    inter = lax.all_to_all(outer, "wide", 0, 0)
+    all_queries = jnp.concatenate(inter, axis=0)
     page_rows = jnp.repeat(jnp.arange(page_count, dtype=jnp.int32), tok_count)
     slot_local = jnp.tile(local_ids, page_count)
     page_offsets = (page_rows - page_rows % 2) * stride_len + page_rows % 2

time: 1150 us -> 1100 us (0.957)
  blocking collectives: 1080 us -> 990 us
  waiting for transfers between devices: 27.2 us -> 51.1 us
  starting transfers between devices: 0.04 us -> 20.1 us
    all_gather x1 -> x0, blocking collectives: 89.3 us -> none  [body(): all_queries = lax.all_gather(own_queries, 'wide', axis=0, tiled=True)]
    all_to_all x0 -> x1, waiting for transfers between devices: none -> 23.9 us  [body(): inter = lax.all_to_all(outer, 'wide', 0, 0)]
    all_to_all x0 -> x1, starting transfers between devices: none -> 20 us  [body(): inter = lax.all_to_all(outer, 'wide', 0, 0)]
  transfers between devices with their start and end apart: 2 -> 3, of which waited for: 1 -> 2; matrix products, arithmetic and copies ran while one was open for 0% -> 1% of each run, Pallas kernels for 0% -> 0%
where the time goes in v1:
time: 1100 us
  blocking collectives  990 us (90%)
  waiting for transfers between devices  51.1 us (5%)
  starting transfers between devices  20.1 us (2%)
  local copies, waits for them, and re-layouts  16.4 us (1%)
  between operations  14.2 us (1%)
    unnamed x1, blocking collectives  492 us
    pmax x1, blocking collectives, body(): best = lax.pmax(max_table, 'wide')  486 us
    reduce_scatter x1, waiting for transfers between devices, body(): lax.psum_scatter(partial_out, 'narrow', scatter_dimension=1, tiled=True)  27.2 us
    all_to_all x1, waiting for transfers between devices, body(): inter = lax.all_to_all(outer, 'wide', 0, 0)  23.9 us
  transfers between devices with their start and end apart: 3, of which 2 were waited for; matrix products, arithmetic and copies ran while one was open for 1% of the time, Pallas kernels for 0%

profile of v1, /device:TPU:8, one launch (start us, length us, event | category | flops | bytes accessed | tf_op | source)
XLA Modules:
  0.0 1103.3 jit_solution(1511308425497121254)
XLA Ops:
  6.5 12.5 %all_gather.3 = bf16[8,1024]{1,0:T(8,128)(2,1)S(1)} all-gather(bf16[8,256]{1,0:T(8,128)(2,1)} %param.8), channel_id=1, replica_groups=mesh['wide'=128,'narrow'=4] {'narrow'}, dimensions={1}, use_global_device_ids=true | all-gather | bytes 20480 | tf_op jit(solution)/shard_map/all_gather | solution.py:33
  19.2 1.5 convolution_convert_fusion
  20.7 0.9 stack.3
  21.6 20.0 %all-to-all-start = ((bf16[128,8,256]{2,1,0:T(8,128)(2,1)}), bf16[128,8,256]{2,1,0:T(8,128)(2,1)}, u32[]{:S(2)}, u32[]{:S(2)}) async-start(bf16[128,8,256]{2,1,0:T(8,128)(2,1)} %stack.3), calls=%async_computation | async-start | bytes 1048576 | tf_op jit(solution)/shard_map/all_to_all | solution.py:60
  41.9 0.8 gather_fusion.2
  42.7 0.7 gather_fusion.3
  43.4 1.9 reshape.253
  45.4 0.7 gather_fusion.4
  46.1 1.8 reshape.254
  48.0 0.7 gather_fusion
  48.7 23.9 %all-to-all-done = bf16[128,8,256]{2,1,0:T(8,128)(2,1)} async-done(((bf16[128,8,256]{2,1,0:T(8,128)(2,1)}), bf16[128,8,256]{2,1,0:T(8,128)(2,1)}, u32[]{:S(2)}, u32[]{:S(2)}) %all-to-all-start) | async-done | bytes 524320 | tf_op jit(solution)/shard_map/all_to_all | solution.py:60
  72.6 1.8 gather_fusion.1
  74.4 2.8 fusion.2
  77.5 0.9 scatter_custom_fusion
  78.3 486.0 %pmax.7 = f32[1024,4]{1,0:T(8,128)S(1)} all-reduce(f32[1024,4]{1,0:T(8,128)S(1)} %scatter_custom_fusion), channel_id=1, replica_groups=mesh['wide'=128,'narrow'=4] {'wide'}, use_global_device_ids=true, to_apply=%region_3.4 | all-reduce | flops 4096 | bytes 32768 | tf_op jit(solution)/shard_map/pmax | solution.py:72
  565.3 2.2 fusion
  567.8 1.8 scatter_custom_fusion.1
  569.9 1.3 dynamic-slice
  571.9 0.9 scatter_custom_fusion.2
  572.8 491.6 %all-reduce.2 = f32[1024,4]{1,0:T(8,128)} all-reduce(f32[1024,4]{1,0:T(8,128)S(1)} %scatter_custom_fusion.2), channel_id=3, replica_groups=mesh['wide'=128,'narrow'=4] {'wide'}, use_global_device_ids=true, to_apply=%region_9.10.clone | all-reduce | flops 4096 | bytes 32768
  1064.4 0.7 fusion.28
  1065.5 2.3 fusion.9
  1067.9 27.2 %reduce-scatter.5.cloned.1.call-done = f32[8,256]{1,0:T(8,128)} async-done(((f32[8,1024]{1,0:T(8,128)}), f32[8,256]{1,0:T(8,128)}) %reduce-scatter.5.cloned.1.call-update) | async-done | bytes 8208 | tf_op jit(solution)/shard_map/reduce_scatter | solution.py:94
  1095.1 1.3 convert_element_type.50
  (48 shorter events, 2.9 us)
Async XLA Ops:
  6.5 36.1 %copy-start = (bf16[64,2,32,256]{3,2,1,0:T(8,128)(2,1)S(1)}, bf16[64,2,32,256]{3,2,1,0:T(8,128)(2,1)}, u32[]{:S(2)}) copy-start(bf16[64,2,32,256]{3,2,1,0:T(8,128)(2,1)} %param.13) | copy-start | bytes 6291460
  6.5 35.3 %copy-start.2 = (s32[1024,8]{0,1:T(8,128)S(1)}, s32[1024,8]{0,1:T(8,128)}, u32[]{:S(2)}) copy-start(s32[1024,8]{0,1:T(8,128)} %param.15) | copy-start | bytes 98308
  21.6 50.9 %all-to-all-start = ((bf16[128,8,256]{2,1,0:T(8,128)(2,1)}), bf16[128,8,256]{2,1,0:T(8,128)(2,1)}, u32[]{:S(2)}, u32[]{:S(2)}) async-start(bf16[128,8,256]{2,1,0:T(8,128)(2,1)} %stack.3), calls=%async_computation | async-start | bytes 1048576 | tf_op jit(solution)/shard_map/all_to_all | solution.py:60
  41.6 1024.0 %reduce-scatter.3.cloned.1.call-start = ((), (), s32[]{:S(2)}) async-start(), calls=%async_computation.3 | async-start | bytes 1056768 | tf_op jit(solution)/shard_map/reduce_scatter | solution.py:80
  46.1 1.9 copy-start.1
  567.7 497.9 %copy-start.3 = (f32[1024]{0:T(1024)S(1)}, f32[1024]{0:T(1024)}, u32[]{:S(2)}) copy-start(f32[1024]{0:T(1024)} %param.9) | copy-start | bytes 12292
  569.7 525.5 %reduce-scatter.5.cloned.1.call-start = ((), (), s32[]{:S(2)}) async-start(), calls=%async_computation.4 | async-start | bytes 40960 | tf_op jit(solution)/shard_map/reduce_scatter | solution.py:94
Sparse Core Ops, SparseCore 0:
  569.8 259.0 reduce-scatter.2
  1068.0 27.0 reduce-scatter.4
